TPU v7x, 256 devices: a whole 4x4x8 slice. The times are simulated.
256 devices in a mesh: dp: 8 (over z), ctx: 32 (over x, y, core).
Axes of the slice: x: 4, y: 4, z: 8, core: 2. Of those that a mesh axis runs over, the one named last changes fastest.
Arguments:
- queries: bfloat16 [8, 4096, 4096], P('dp', 'ctx'), may hold values from -120 to 120
- layer_input: bfloat16 [8, 4096, 4096], P('dp', 'ctx'), may hold values from -6 to 6
- key_value_weight: bfloat16 [4096, 1024], P(('dp', 'ctx')), may hold values from -0.25 to 0.25
- output_gradient: bfloat16 [8, 4096, 4096], P('dp', 'ctx'), may hold values from -6 to 6
- document_lengths: int32 [8, 32], P('dp'), may hold values from 1 to 1024, 4096 in all within a row
Outputs:
- attended: bfloat16 [8, 4096, 4096], P('dp', 'ctx')
- query_grad: bfloat16 [8, 4096, 4096], P('dp', 'ctx')
- input_grad: bfloat16 [8, 4096, 4096], P('dp', 'ctx')
Inputs may be any that keep to these rules, and one draw needn't show every extreme that they name: `document_lengths`: each row holds the lengths of the 32 documents of one sequence in order; they sum to 4096, and one of them is exactly 1024.
All inputs are finite; a program needn't handle non-finite values.
Results may differ from a plain program's by a relative error of at most 0.02.
The roundings to bfloat16 on the way count: a program that leaves them out, or rounds other values in their place, can miss the bound.
Values may be sent and summed in bfloat16 or wider, within the bound.
A program may use at most 128 MiB of HBM per device.

v0:
```python
import math
import jax
import jax.numpy as jnp
from jax import lax
from jax.sharding import PartitionSpec as P

QUERY_HEADS = 32
KEY_VALUE_HEADS = 4
HEAD_SIZE = 128
masked_score = -1e30


def from_behind(value, axis, steps):
    count = lax.axis_size(axis)
    first, last = (max(0, -steps), min(count, count - steps))
    return lax.ppermute(value, axis, [(source, source + steps) for source in range(first, last)])


def document_of(positions, ends):
    return jnp.sum((positions[..., None] >= ends).astype(jnp.int32), axis=-1)


def attend(query_tile_block, gradient_block, key_blocks, query_start, key_starts, ends):
    row_indices = query_tile_block.shape[0]
    width = query_tile_block.shape[-1]
    heads = query_tile_block.shape[1]
    head_group = query_tile_block.shape[2]
    count = key_blocks.shape[1]
    scale = 1.0 / math.sqrt(width)
    query_start = jnp.asarray(query_start, jnp.int32)
    query_pos = query_start + jnp.arange(row_indices, dtype=jnp.int32)
    query_doc = document_of(query_pos, ends)
    first_doc = document_of(query_start, ends)
    last_query = query_start + row_indices - 1

    def mask_of(key_start):
        key_pos = key_start + jnp.arange(count, dtype=jnp.int32)
        key_doc = document_of(key_pos, ends)
        allowed = (
            (query_doc[:, None] == key_doc[None, :])
            & (key_pos[None, :] <= query_pos[:, None])
            & (key_pos[None, :] >= 0)
        )
        last_key = jnp.minimum(key_start + count - 1, last_query)
        live = (
            (key_start <= last_query)
            & (key_start + count - 1 >= 0)
            & (document_of(last_key, ends) >= first_doc)
        )
        return (allowed, live)

    def scores(block_slice):
        return scale * jnp.einsum(
            "qhgd,khd->hgqk",
            query_tile_block,
            block_slice[..., :width],
            preferred_element_type=jnp.float32,
        )

    def forward_step(state, item):
        block_slice, key_start = item
        allowed, live = mask_of(key_start)

        def forward(state):
            highest, total, accum = state
            score = scores(block_slice)
            newest = jnp.maximum(highest, jnp.max(jnp.where(allowed, score, masked_score), axis=-1))
            weight = jnp.exp(jnp.where(allowed, score - newest[..., None], masked_score))
            factor = jnp.exp(highest - newest)
            total = total * factor + jnp.sum(weight, axis=-1)
            mixed = jnp.einsum(
                "hgqk,khd->qhgd",
                weight.astype(jnp.bfloat16),
                block_slice[..., width:],
                preferred_element_type=jnp.float32,
            )
            accum = accum * jnp.transpose(factor, (2, 0, 1))[..., None] + mixed
            return (newest, total, accum)

        return (lax.cond(live, forward, lambda kept: kept, state), None)

    state = (
        jnp.full((heads, head_group, row_indices), masked_score, jnp.float32),
        jnp.zeros((heads, head_group, row_indices), jnp.float32),
        jnp.zeros(query_tile_block.shape, jnp.float32),
    )
    state, unused = lax.scan(forward_step, state, (key_blocks, key_starts))
    highest, total, accum = state
    output = (accum / jnp.transpose(total, (2, 0, 1))[..., None]).astype(jnp.bfloat16)
    logsum = highest + jnp.log(total)
    product = jnp.transpose(
        jnp.sum(gradient_block.astype(jnp.float32) * output.astype(jnp.float32), axis=-1), (1, 2, 0)
    )

    def backward_step(query_sum, item):
        block_slice, key_start = item
        allowed, live = mask_of(key_start)

        def backward(query_sum):
            score = scores(block_slice)
            prob = jnp.exp(jnp.where(allowed, score - logsum[..., None], masked_score))
            pressure = jnp.einsum(
                "qhgd,khd->hgqk",
                gradient_block,
                block_slice[..., width:],
                preferred_element_type=jnp.float32,
            )
            slope = (prob * (pressure - product[..., None])).astype(jnp.bfloat16)
            query_sum = query_sum + jnp.einsum(
                "hgqk,khd->qhgd",
                slope,
                block_slice[..., :width],
                preferred_element_type=jnp.float32,
            )
            key_part = scale * jnp.einsum(
                "hgqk,qhgd->khd", slope, query_tile_block, preferred_element_type=jnp.float32
            )
            value_part = jnp.einsum(
                "hgqk,qhgd->khd",
                prob.astype(jnp.bfloat16),
                gradient_block,
                preferred_element_type=jnp.float32,
            )
            return (query_sum, jnp.concatenate([key_part, value_part], axis=-1))

        def skipped(query_sum):
            return (query_sum, jnp.zeros(block_slice.shape, jnp.float32))

        return lax.cond(live, backward, skipped, query_sum)

    query_sum, pieces = lax.scan(
        backward_step, jnp.zeros(query_tile_block.shape, jnp.float32), (key_blocks, key_starts)
    )
    return (output, (scale * query_sum).astype(jnp.bfloat16), pieces)


def shards(queries, layer_input, key_value_weight, output_gradient, document_lengths):
    inputs = layer_input[0]
    row_indices = inputs.shape[0]
    ends = jnp.cumsum(document_lengths[0])
    columns_all = key_value_weight.shape[1]
    half_length = columns_all // 2
    projected_input = jnp.dot(
        inputs,
        lax.all_gather(key_value_weight, ("dp", "ctx"), axis=0, tiled=True),
        preferred_element_type=jnp.float32,
    )
    projected_input = projected_input.astype(jnp.bfloat16)
    key_rows = projected_input[:, :half_length].reshape(row_indices, KEY_VALUE_HEADS, HEAD_SIZE)
    value_rows = projected_input[:, half_length:].reshape(row_indices, KEY_VALUE_HEADS, HEAD_SIZE)
    paired = jnp.concatenate([key_rows, value_rows], axis=-1)
    devices = lax.axis_size("ctx")
    window_reach = devices // 4
    head_group = QUERY_HEADS // KEY_VALUE_HEADS
    offsets = jnp.arange(window_reach + 1, dtype=jnp.int32) * row_indices
    query_tile_block = queries[0].reshape(row_indices, KEY_VALUE_HEADS, head_group, HEAD_SIZE)
    gradient_block = output_gradient[0].reshape(row_indices, KEY_VALUE_HEADS, head_group, HEAD_SIZE)
    start = lax.axis_index("ctx") * row_indices
    blocks = [paired]
    for offset in range(window_reach):
        blocks.append(from_behind(blocks[-1], "ctx", 1))
    stacked = jnp.stack(blocks)
    output, query_sum, pieces = attend(
        query_tile_block, gradient_block, stacked, start, start - offsets, ends
    )
    carried = pieces[window_reach]
    for offset in range(window_reach - 1, -1, -1):
        carried = from_behind(carried, "ctx", -1) + pieces[offset]
    attended = output.reshape(row_indices, QUERY_HEADS * HEAD_SIZE)
    query_grad = query_sum.reshape(row_indices, QUERY_HEADS * HEAD_SIZE)
    gradient_value = carried.astype(jnp.bfloat16)
    flat = jnp.concatenate(
        [
            gradient_value[..., :HEAD_SIZE].reshape(row_indices, KEY_VALUE_HEADS * HEAD_SIZE),
            gradient_value[..., HEAD_SIZE:].reshape(row_indices, KEY_VALUE_HEADS * HEAD_SIZE),
        ],
        axis=1,
    )
    input_grad = lax.dot_general(
        flat,
        lax.all_gather(key_value_weight, ("dp", "ctx"), axis=0, tiled=True),
        (((1,), (1,)), ((), ())),
        preferred_element_type=jnp.float32,
    )
    return (attended[None], query_grad[None], input_grad.astype(jnp.bfloat16)[None])


def solution(mesh):
    return jax.shard_map(
        shards,
        mesh=mesh,
        in_specs=(
            P("dp", "ctx", None),
            P("dp", "ctx", None),
            P(("dp", "ctx"), None),
            P("dp", "ctx", None),
            P("dp", None),
        ),
        out_specs=(P("dp", "ctx", None), P("dp", "ctx", None), P("dp", "ctx", None)),
        check_vma=False,
    )
```

profile of v0, /device:TPU:57, one launch (start us, length us, event | category | flops | bytes accessed | tf_op | source)
XLA Modules:
  0.0 591.8 jit_solution(6829735065192717386)
XLA Ops:
  7.9 123.9 %all-gather.2.cloned.1.call-done = bf16[4096,1024]{1,0:T(8,128)(2,1)} async-done(((bf16[16,1024]{1,0:T(8,128)(2,1)}), bf16[4096,1024]{1,0:T(8,128)(2,1)}) %all-gather.2.cloned.1.call-update) | async-done | bytes 8388624 | tf_op jit(solution)/shard_map/all_gather | solution.py:145
  131.9 4.6 convolution_convert_fusion.1
  136.6 2.9 collective-permute-start
  139.5 3.3 collective-permute-done
  142.8 6.5 %collective-permute-start.1 = (bf16[128,4,256]{2,0,1:T(8,128)(2,1)S(1)}, bf16[128,4,256]{2,0,1:T(8,128)(2,1)S(1)}, u32[]{:S(2)}, u32[]{:S(2)}) collective-permute-start(bf16[128,4,256]{2,0,1:T(8,128)(2,1)S(1)} %collective-permute-done), channel_id=1, source_target_pairs={{0,1},{1,2},{2,3},{3,4},{4,5},{5,6},{6,7},{7,8},{8,9},{9,10},{10,1... | collective-permute-start | bytes 786440 | tf_op jit(solution)/shard_map/ppermute | solution.py:16
  149.3 3.3 collective-permute-done.1
  152.6 6.5 %collective-permute-start.2 = (bf16[128,4,256]{2,0,1:T(8,128)(2,1)S(1)}, bf16[128,4,256]{2,0,1:T(8,128)(2,1)}, u32[]{:S(2)}, u32[]{:S(2)}) collective-permute-start(bf16[128,4,256]{2,0,1:T(8,128)(2,1)S(1)} %collective-permute-done.1), channel_id=1, source_target_pairs={{0,1},{1,2},{2,3},{3,4},{4,5},{5,6},{6,7},{7,8},{8,9},{9,10},{10,1... | collective-permute-start | bytes 786440 | tf_op jit(solution)/shard_map/ppermute | solution.py:16
  159.1 3.3 collective-permute-done.2
  162.4 6.6 %collective-permute-start.3 = (bf16[128,4,256]{2,0,1:T(8,128)(2,1)}, bf16[128,4,256]{2,0,1:T(8,128)(2,1)}, u32[]{:S(2)}, u32[]{:S(2)}) collective-permute-start(bf16[128,4,256]{2,0,1:T(8,128)(2,1)} %collective-permute-done.2), channel_id=1, source_target_pairs={{0,1},{1,2},{2,3},{3,4},{4,5},{5,6},{6,7},{7,8},{8,9},{9,10},{10,1... | collective-permute-start | bytes 786440 | tf_op jit(solution)/shard_map/ppermute | solution.py:16
  173.6 5.5 collective-permute-start.4
  182.7 6.4 %collective-permute-start.5 = (bf16[128,4,256]{2,0,1:T(8,128)(2,1)S(1)}, bf16[128,4,256]{2,0,1:T(8,128)(2,1)S(1)}, u32[]{:S(2)}, u32[]{:S(2)}) collective-permute-start(bf16[128,4,256]{2,0,1:T(8,128)(2,1)S(1)} %collective-permute-done.4), channel_id=1, source_target_pairs={{0,1},{1,2},{2,3},{3,4},{4,5},{5,6},{6,7},{7,8},{8,9},{9,10},{10,1... | collective-permute-start | bytes 786440 | tf_op jit(solution)/shard_map/ppermute | solution.py:16
  192.4 6.4 %collective-permute-start.6 = (bf16[128,4,256]{2,0,1:T(8,128)(2,1)S(1)}, bf16[128,4,256]{2,0,1:T(8,128)(2,1)S(1)}, u32[]{:S(2)}, u32[]{:S(2)}) collective-permute-start(bf16[128,4,256]{2,0,1:T(8,128)(2,1)S(1)} %collective-permute-done.5), channel_id=1, source_target_pairs={{0,1},{1,2},{2,3},{3,4},{4,5},{5,6},{6,7},{7,8},{8,9},{9,10},{10,1... | collective-permute-start | bytes 786440 | tf_op jit(solution)/shard_map/ppermute | solution.py:16
  202.2 6.5 %collective-permute-start.7 = (bf16[128,4,256]{2,0,1:T(8,128)(2,1)S(1)}, bf16[128,4,256]{2,0,1:T(8,128)(2,1)S(1)}, u32[]{:S(2)}, u32[]{:S(2)}) collective-permute-start(bf16[128,4,256]{2,0,1:T(8,128)(2,1)S(1)} %collective-permute-done.6), channel_id=1, source_target_pairs={{0,1},{1,2},{2,3},{3,4},{4,5},{5,6},{6,7},{7,8},{8,9},{9,10},{10,1... | collective-permute-start | bytes 786440 | tf_op jit(solution)/shard_map/ppermute | solution.py:16
  214.2 101.9 %while.39 = (s32[]{:T(128)}, f32[4,8,128]{2,1,0:T(8,128)S(1)}, f32[4,8,128]{2,1,0:T(8,128)S(1)}, f32[128,4,8,128]{3,0,2,1:T(8,128)}, s32[9]{0:T(128)S(1)}, /*ind...) while((s32[]{:T(128)}, f32[4,8,128]{2,1,0:T(8,128)S(1)}, ...), condition=%wide.region_10.11_spmd.clone, body=%wide.region_3.10_spmd.clone.sunk | while | flops 275341920 | bytes 29466576 | solution.py:87
  218.8 7.6 %conditional.6 = ((f32[4,8,128]{2,1,0:T(8,128)S(1)}, f32[4,8,128]{2,1,0:T(8,128)S(1)}, f32[128,4,8,128]{3,0,2,1:T(8,128)})) conditional(s32[]{:T(128)} %convert_element_type.143, (f32[4,8,128]{2,1,0:T(8,128)S(1)}, f32[4,8,128]{2,1,0:T(8,128)S(1)}, f32[128,4,8,128]{3,0,2,1:T(8,128)}) %tuple.123, (s32[128]{0:T(128)S(1)}, s32[128,32]{1,0:T(8,128)S(1)}, ...), branch_computations={%region_5.5_spmd, %region_6.9_spmd} | conditional | flops 275333504 | bytes 29447532 | solution.py:80
  230.9 7.6 %conditional.6 = ((f32[4,8,128]{2,1,0:T(8,128)S(1)}, f32[4,8,128]{2,1,0:T(8,128)S(1)}, f32[128,4,8,128]{3,0,2,1:T(8,128)})) conditional(s32[]{:T(128)} %convert_element_type.143, (f32[4,8,128]{2,1,0:T(8,128)S(1)}, f32[4,8,128]{2,1,0:T(8,128)S(1)}, f32[128,4,8,128]{3,0,2,1:T(8,128)}) %tuple.123, (s32[128]{0:T(128)S(1)}, s32[128,32]{1,0:T(8,128)S(1)}, ...), branch_computations={%region_5.5_spmd, %region_6.9_spmd} | conditional | flops 275333504 | bytes 29447532 | solution.py:80
  233.5 1.8 fusion.4
  243.1 7.6 %conditional.6 = ((f32[4,8,128]{2,1,0:T(8,128)S(1)}, f32[4,8,128]{2,1,0:T(8,128)S(1)}, f32[128,4,8,128]{3,0,2,1:T(8,128)})) conditional(s32[]{:T(128)} %convert_element_type.143, (f32[4,8,128]{2,1,0:T(8,128)S(1)}, f32[4,8,128]{2,1,0:T(8,128)S(1)}, f32[128,4,8,128]{3,0,2,1:T(8,128)}) %tuple.123, (s32[128]{0:T(128)S(1)}, s32[128,32]{1,0:T(8,128)S(1)}, ...), branch_computations={%region_5.5_spmd, %region_6.9_spmd} | conditional | flops 275333504 | bytes 29447532 | solution.py:80
  245.7 1.8 fusion.4
  255.3 7.6 %conditional.6 = ((f32[4,8,128]{2,1,0:T(8,128)S(1)}, f32[4,8,128]{2,1,0:T(8,128)S(1)}, f32[128,4,8,128]{3,0,2,1:T(8,128)})) conditional(s32[]{:T(128)} %convert_element_type.143, (f32[4,8,128]{2,1,0:T(8,128)S(1)}, f32[4,8,128]{2,1,0:T(8,128)S(1)}, f32[128,4,8,128]{3,0,2,1:T(8,128)}) %tuple.123, (s32[128]{0:T(128)S(1)}, s32[128,32]{1,0:T(8,128)S(1)}, ...), branch_computations={%region_5.5_spmd, %region_6.9_spmd} | conditional | flops 275333504 | bytes 29447532 | solution.py:80
  267.5 7.6 %conditional.6 = ((f32[4,8,128]{2,1,0:T(8,128)S(1)}, f32[4,8,128]{2,1,0:T(8,128)S(1)}, f32[128,4,8,128]{3,0,2,1:T(8,128)})) conditional(s32[]{:T(128)} %convert_element_type.143, (f32[4,8,128]{2,1,0:T(8,128)S(1)}, f32[4,8,128]{2,1,0:T(8,128)S(1)}, f32[128,4,8,128]{3,0,2,1:T(8,128)}) %tuple.123, (s32[128]{0:T(128)S(1)}, s32[128,32]{1,0:T(8,128)S(1)}, ...), branch_computations={%region_5.5_spmd, %region_6.9_spmd} | conditional | flops 275333504 | bytes 29447532 | solution.py:80
  279.6 7.6 %conditional.6 = ((f32[4,8,128]{2,1,0:T(8,128)S(1)}, f32[4,8,128]{2,1,0:T(8,128)S(1)}, f32[128,4,8,128]{3,0,2,1:T(8,128)})) conditional(s32[]{:T(128)} %convert_element_type.143, (f32[4,8,128]{2,1,0:T(8,128)S(1)}, f32[4,8,128]{2,1,0:T(8,128)S(1)}, f32[128,4,8,128]{3,0,2,1:T(8,128)}) %tuple.123, (s32[128]{0:T(128)S(1)}, s32[128,32]{1,0:T(8,128)S(1)}, ...), branch_computations={%region_5.5_spmd, %region_6.9_spmd} | conditional | flops 275333504 | bytes 29447532 | solution.py:80
  282.2 1.8 fusion.4
  291.8 7.6 %conditional.6 = ((f32[4,8,128]{2,1,0:T(8,128)S(1)}, f32[4,8,128]{2,1,0:T(8,128)S(1)}, f32[128,4,8,128]{3,0,2,1:T(8,128)})) conditional(s32[]{:T(128)} %convert_element_type.143, (f32[4,8,128]{2,1,0:T(8,128)S(1)}, f32[4,8,128]{2,1,0:T(8,128)S(1)}, f32[128,4,8,128]{3,0,2,1:T(8,128)}) %tuple.123, (s32[128]{0:T(128)S(1)}, s32[128,32]{1,0:T(8,128)S(1)}, ...), branch_computations={%region_5.5_spmd, %region_6.9_spmd} | conditional | flops 275333504 | bytes 29447532 | solution.py:80
  304.0 7.6 %conditional.6 = ((f32[4,8,128]{2,1,0:T(8,128)S(1)}, f32[4,8,128]{2,1,0:T(8,128)S(1)}, f32[128,4,8,128]{3,0,2,1:T(8,128)})) conditional(s32[]{:T(128)} %convert_element_type.143, (f32[4,8,128]{2,1,0:T(8,128)S(1)}, f32[4,8,128]{2,1,0:T(8,128)S(1)}, f32[128,4,8,128]{3,0,2,1:T(8,128)}) %tuple.123, (s32[128]{0:T(128)S(1)}, s32[128,32]{1,0:T(8,128)S(1)}, ...), branch_computations={%region_5.5_spmd, %region_6.9_spmd} | conditional | flops 275333504 | bytes 29447532 | solution.py:80
  316.2 2.9 copy.49
  319.1 3.0 multiply_reduce_fusion
  323.7 125.9 %while.40 = (s32[]{:T(128)}, f32[128,4,8,128]{3,0,2,1:T(8,128)}, f32[9,128,4,256]{1,3,2,0:T(8,128)}, s32[9]{0:T(128)S(1)}, s32[]{:T(128)}, /*index=5*/s32[32]{0:...) while((s32[]{:T(128)}, f32[128,4,8,128]{3,0,2,1:T(8,128)}, ...), condition=%wide.region_17.18_spmd.clone, body=%wide.region_12.17_spmd.clone.sunk | while | flops 675558016 | bytes 38248896 | solution.py:131
  328.4 8.2 %conditional.7 = (f32[128,4,8,128]{3,0,2,1:T(8,128)}, f32[1,128,4,256]{1,3,2,0:T(8,128)}) conditional(s32[]{:T(128)} %convert_element_type.146, f32[128,4,8,128]{3,0,2,1:T(8,128)} %get-tuple-element.1136, (s32[128]{0:T(128)S(1)}, s32[128,32]{1,0:T(8,128)S(1)}, s32[]{:T(128)}, s32[1,128]{1,0:T(1,128)S(1)}, s32[]{:T(128)}, ...), branch_computations={%region_14.14_spmd, %region_15.16_spmd} | conditional | flops 675549568 | bytes 37180764 | solution.py:129
  336.6 1.9 constant_dynamic-update-slice_fusion.2
  343.3 8.2 %conditional.7 = (f32[128,4,8,128]{3,0,2,1:T(8,128)}, f32[1,128,4,256]{1,3,2,0:T(8,128)}) conditional(s32[]{:T(128)} %convert_element_type.146, f32[128,4,8,128]{3,0,2,1:T(8,128)} %get-tuple-element.1136, (s32[128]{0:T(128)S(1)}, s32[128,32]{1,0:T(8,128)S(1)}, s32[]{:T(128)}, s32[1,128]{1,0:T(1,128)S(1)}, s32[]{:T(128)}, ...), branch_computations={%region_14.14_spmd, %region_15.16_spmd} | conditional | flops 675549568 | bytes 37180764 | solution.py:129
  351.5 1.9 constant_dynamic-update-slice_fusion.2
  358.1 8.2 %conditional.7 = (f32[128,4,8,128]{3,0,2,1:T(8,128)}, f32[1,128,4,256]{1,3,2,0:T(8,128)}) conditional(s32[]{:T(128)} %convert_element_type.146, f32[128,4,8,128]{3,0,2,1:T(8,128)} %get-tuple-element.1136, (s32[128]{0:T(128)S(1)}, s32[128,32]{1,0:T(8,128)S(1)}, s32[]{:T(128)}, s32[1,128]{1,0:T(1,128)S(1)}, s32[]{:T(128)}, ...), branch_computations={%region_14.14_spmd, %region_15.16_spmd} | conditional | flops 675549568 | bytes 37180764 | solution.py:129
  366.3 1.9 constant_dynamic-update-slice_fusion.2
  372.9 8.2 %conditional.7 = (f32[128,4,8,128]{3,0,2,1:T(8,128)}, f32[1,128,4,256]{1,3,2,0:T(8,128)}) conditional(s32[]{:T(128)} %convert_element_type.146, f32[128,4,8,128]{3,0,2,1:T(8,128)} %get-tuple-element.1136, (s32[128]{0:T(128)S(1)}, s32[128,32]{1,0:T(8,128)S(1)}, s32[]{:T(128)}, s32[1,128]{1,0:T(1,128)S(1)}, s32[]{:T(128)}, ...), branch_computations={%region_14.14_spmd, %region_15.16_spmd} | conditional | flops 675549568 | bytes 37180764 | solution.py:129
  381.1 1.9 constant_dynamic-update-slice_fusion.2
  387.7 8.2 %conditional.7 = (f32[128,4,8,128]{3,0,2,1:T(8,128)}, f32[1,128,4,256]{1,3,2,0:T(8,128)}) conditional(s32[]{:T(128)} %convert_element_type.146, f32[128,4,8,128]{3,0,2,1:T(8,128)} %get-tuple-element.1136, (s32[128]{0:T(128)S(1)}, s32[128,32]{1,0:T(8,128)S(1)}, s32[]{:T(128)}, s32[1,128]{1,0:T(1,128)S(1)}, s32[]{:T(128)}, ...), branch_computations={%region_14.14_spmd, %region_15.16_spmd} | conditional | flops 675549568 | bytes 37180764 | solution.py:129
  395.9 1.9 constant_dynamic-update-slice_fusion.2
  402.5 8.2 %conditional.7 = (f32[128,4,8,128]{3,0,2,1:T(8,128)}, f32[1,128,4,256]{1,3,2,0:T(8,128)}) conditional(s32[]{:T(128)} %convert_element_type.146, f32[128,4,8,128]{3,0,2,1:T(8,128)} %get-tuple-element.1136, (s32[128]{0:T(128)S(1)}, s32[128,32]{1,0:T(8,128)S(1)}, s32[]{:T(128)}, s32[1,128]{1,0:T(1,128)S(1)}, s32[]{:T(128)}, ...), branch_computations={%region_14.14_spmd, %region_15.16_spmd} | conditional | flops 675549568 | bytes 37180764 | solution.py:129
  410.7 1.9 constant_dynamic-update-slice_fusion.2
  417.3 8.2 %conditional.7 = (f32[128,4,8,128]{3,0,2,1:T(8,128)}, f32[1,128,4,256]{1,3,2,0:T(8,128)}) conditional(s32[]{:T(128)} %convert_element_type.146, f32[128,4,8,128]{3,0,2,1:T(8,128)} %get-tuple-element.1136, (s32[128]{0:T(128)S(1)}, s32[128,32]{1,0:T(8,128)S(1)}, s32[]{:T(128)}, s32[1,128]{1,0:T(1,128)S(1)}, s32[]{:T(128)}, ...), branch_computations={%region_14.14_spmd, %region_15.16_spmd} | conditional | flops 675549568 | bytes 37180764 | solution.py:129
  425.5 1.9 constant_dynamic-update-slice_fusion.2
  432.1 8.2 %conditional.7 = (f32[128,4,8,128]{3,0,2,1:T(8,128)}, f32[1,128,4,256]{1,3,2,0:T(8,128)}) conditional(s32[]{:T(128)} %convert_element_type.146, f32[128,4,8,128]{3,0,2,1:T(8,128)} %get-tuple-element.1136, (s32[128]{0:T(128)S(1)}, s32[128,32]{1,0:T(8,128)S(1)}, s32[]{:T(128)}, s32[1,128]{1,0:T(1,128)S(1)}, s32[]{:T(128)}, ...), branch_computations={%region_14.14_spmd, %region_15.16_spmd} | conditional | flops 675549568 | bytes 37180764 | solution.py:129
  440.2 1.9 constant_dynamic-update-slice_fusion.2
  447.7 1.9 constant_dynamic-update-slice_fusion.2
  450.7 1.9 collective-permute-start.8
  452.6 26.4 %collective-permute-done.8 = f32[128,4,256]{0,2,1:T(8,128)S(1)} collective-permute-done((f32[128,4,256]{0,2,1:T(8,128)S(1)}, f32[128,4,256]{0,2,1:T(8,128)S(1)}, u32[]{:S(2)}, u32[]{:S(2)}) %collective-permute-start.8) | collective-permute-done | bytes 524320 | tf_op jit(solution)/shard_map/ppermute | solution.py:16
  480.1 1.9 collective-permute-start.9
  482.0 10.7 %collective-permute-done.9 = f32[128,4,256]{0,2,1:T(8,128)S(1)} collective-permute-done((f32[128,4,256]{0,2,1:T(8,128)S(1)}, f32[128,4,256]{0,2,1:T(8,128)S(1)}, u32[]{:S(2)}, u32[]{:S(2)}) %collective-permute-start.9) | collective-permute-done | bytes 524320 | tf_op jit(solution)/shard_map/ppermute | solution.py:16
  493.9 1.9 collective-permute-start.10
  495.8 10.7 %collective-permute-done.10 = f32[128,4,256]{0,2,1:T(8,128)S(1)} collective-permute-done((f32[128,4,256]{0,2,1:T(8,128)S(1)}, f32[128,4,256]{0,2,1:T(8,128)S(1)}, u32[]{:S(2)}, u32[]{:S(2)}) %collective-permute-start.10) | collective-permute-done | bytes 524320 | tf_op jit(solution)/shard_map/ppermute | solution.py:16
  507.6 1.9 collective-permute-start.11
  509.5 10.7 %collective-permute-done.11 = f32[128,4,256]{0,2,1:T(8,128)S(1)} collective-permute-done((f32[128,4,256]{0,2,1:T(8,128)S(1)}, f32[128,4,256]{0,2,1:T(8,128)S(1)}, u32[]{:S(2)}, u32[]{:S(2)}) %collective-permute-start.11) | collective-permute-done | bytes 524320 | tf_op jit(solution)/shard_map/ppermute | solution.py:16
  521.3 1.9 collective-permute-start.12
  523.2 10.7 %collective-permute-done.12 = f32[128,4,256]{0,2,1:T(8,128)S(1)} collective-permute-done((f32[128,4,256]{0,2,1:T(8,128)S(1)}, f32[128,4,256]{0,2,1:T(8,128)S(1)}, u32[]{:S(2)}, u32[]{:S(2)}) %collective-permute-start.12) | collective-permute-done | bytes 524320 | tf_op jit(solution)/shard_map/ppermute | solution.py:16
  535.0 1.9 collective-permute-start.13
  537.0 10.7 %collective-permute-done.13 = f32[128,4,256]{0,2,1:T(8,128)S(1)} collective-permute-done((f32[128,4,256]{0,2,1:T(8,128)S(1)}, f32[128,4,256]{0,2,1:T(8,128)S(1)}, u32[]{:S(2)}, u32[]{:S(2)}) %collective-permute-start.13) | collective-permute-done | bytes 524320 | tf_op jit(solution)/shard_map/ppermute | solution.py:16
  548.8 2.1 collective-permute-start.14
  550.9 10.7 %collective-permute-done.14 = f32[128,4,256]{0,2,1:T(8,128)S(1)} collective-permute-done((f32[128,4,256]{0,2,1:T(8,128)S(1)}, f32[128,4,256]{0,2,1:T(8,128)S(1)}, u32[]{:S(2)}, u32[]{:S(2)}) %collective-permute-start.14) | collective-permute-done | bytes 524320 | tf_op jit(solution)/shard_map/ppermute | solution.py:16
  561.5 1.9 bitcast_add_fusion.3
  563.5 2.1 collective-permute-start.15
  565.6 2.3 copy.65
  570.1 6.3 %collective-permute-done.15 = f32[128,4,256]{0,2,1:T(8,128)} collective-permute-done((f32[128,4,256]{0,2,1:T(8,128)}, f32[128,4,256]{0,2,1:T(8,128)}, u32[]{:S(2)}, u32[]{:S(2)}) %collective-permute-start.15) | collective-permute-done | bytes 524320 | tf_op jit(solution)/shard_map/ppermute | solution.py:16
  577.7 7.3 %fusion.27 = bf16[1,128,4096]{2,1,0:T(8,128)(2,1)} fusion(bf16[4096,1024]{1,0:T(8,128)(2,1)} %all-gather.2.cloned.1.call-done, bf16[128,512]{0,1:T(8,128)(2,1)S(1)} %bitcast.167, bf16[128,512]{0,1:T(8,128)(2,1)S(1)} %bitcast.166), kind=kOutput, calls=%fused_computation.57 | convolution fusion | flops 1074790400 | bytes 9699328 | tf_op jit(solution)/shard_map/dot_general | solution.py:179
  (423 shorter events, 191.6 us)
Async XLA Ops:
  7.2 124.7 %copy-start = (bf16[1,128,4096]{2,1,0:T(8,128)(2,1)S(1)}, bf16[1,128,4096]{2,1,0:T(8,128)(2,1)}, u32[]{:S(2)}) copy-start(bf16[1,128,4096]{2,1,0:T(8,128)(2,1)} %param.14) | copy-start | bytes 3145732
  7.2 124.7 %all-gather.2.cloned.1.call-start = ((), (), s32[]{:S(2)}) async-start(), calls=%async_computation | async-start | bytes 8421376 | tf_op jit(solution)/shard_map/all_gather | solution.py:145
  7.9 161.1 %copy-start.9 = (s32[1,32]{1,0:T(1,128)S(1)}, s32[1,32]{1,0:T(1,128)}, u32[]{:S(2)}) copy-start(s32[1,32]{1,0:T(1,128)} %param.17) | copy-start | bytes 388
  7.9 161.4 %copy-start.6 = (bf16[1,128,4096]{2,1,0:T(8,128)(2,1)S(1)}, bf16[1,128,4096]{2,1,0:T(8,128)(2,1)}, u32[]{:S(2)}) copy-start(bf16[1,128,4096]{2,1,0:T(8,128)(2,1)} %param.13) | copy-start | bytes 3145732
  136.6 6.2 %collective-permute-start = (bf16[128,4,256]{2,0,1:T(8,128)(2,1)S(1)}, bf16[128,4,256]{2,0,1:T(8,128)(2,1)S(1)}, u32[]{:S(2)}, u32[]{:S(2)}) collective-permute-start(bf16[128,4,256]{2,0,1:T(8,128)(2,1)S(1)} %bitcast_dynamic-update-slice_fusion.9), channel_id=1, source_target_pairs={{0,1},{1,2},{2,3},{3,4},{4,5},{5,6},{6,7},{7,8},{8,9},{9,10},{10,1... | collective-permute-start | bytes 786440 | tf_op jit(solution)/shard_map/ppermute | solution.py:16
  142.8 26.4 %copy-start.8 = (bf16[128,4,256]{2,0,1:T(8,128)(2,1)}, bf16[128,4,256]{2,0,1:T(8,128)(2,1)S(1)}, u32[]{:S(2)}) copy-start(bf16[128,4,256]{2,0,1:T(8,128)(2,1)S(1)} %collective-permute-done) | copy-start | bytes 786436
  142.8 9.8 %collective-permute-start.1 = (bf16[128,4,256]{2,0,1:T(8,128)(2,1)S(1)}, bf16[128,4,256]{2,0,1:T(8,128)(2,1)S(1)}, u32[]{:S(2)}, u32[]{:S(2)}) collective-permute-start(bf16[128,4,256]{2,0,1:T(8,128)(2,1)S(1)} %collective-permute-done), channel_id=1, source_target_pairs={{0,1},{1,2},{2,3},{3,4},{4,5},{5,6},{6,7},{7,8},{8,9},{9,10},{10,1... | collective-permute-start | bytes 786440 | tf_op jit(solution)/shard_map/ppermute | solution.py:16
  152.6 16.6 %copy-start.7 = (bf16[128,4,256]{2,0,1:T(8,128)(2,1)}, bf16[128,4,256]{2,0,1:T(8,128)(2,1)S(1)}, u32[]{:S(2)}) copy-start(bf16[128,4,256]{2,0,1:T(8,128)(2,1)S(1)} %collective-permute-done.1) | copy-start | bytes 786436
  152.6 9.8 %collective-permute-start.2 = (bf16[128,4,256]{2,0,1:T(8,128)(2,1)S(1)}, bf16[128,4,256]{2,0,1:T(8,128)(2,1)}, u32[]{:S(2)}, u32[]{:S(2)}) collective-permute-start(bf16[128,4,256]{2,0,1:T(8,128)(2,1)S(1)} %collective-permute-done.1), channel_id=1, source_target_pairs={{0,1},{1,2},{2,3},{3,4},{4,5},{5,6},{6,7},{7,8},{8,9},{9,10},{10,1... | collective-permute-start | bytes 786440 | tf_op jit(solution)/shard_map/ppermute | solution.py:16
  162.4 11.2 %collective-permute-start.3 = (bf16[128,4,256]{2,0,1:T(8,128)(2,1)}, bf16[128,4,256]{2,0,1:T(8,128)(2,1)}, u32[]{:S(2)}, u32[]{:S(2)}) collective-permute-start(bf16[128,4,256]{2,0,1:T(8,128)(2,1)} %collective-permute-done.2), channel_id=1, source_target_pairs={{0,1},{1,2},{2,3},{3,4},{4,5},{5,6},{6,7},{7,8},{8,9},{9,10},{10,1... | collective-permute-start | bytes 786440 | tf_op jit(solution)/shard_map/ppermute | solution.py:16
  173.6 9.1 %collective-permute-start.4 = (bf16[128,4,256]{2,0,1:T(8,128)(2,1)}, bf16[128,4,256]{2,0,1:T(8,128)(2,1)S(1)}, u32[]{:S(2)}, u32[]{:S(2)}) collective-permute-start(bf16[128,4,256]{2,0,1:T(8,128)(2,1)} %collective-permute-done.3), channel_id=1, source_target_pairs={{0,1},{1,2},{2,3},{3,4},{4,5},{5,6},{6,7},{7,8},{8,9},{9,10},{10,1... | collective-permute-start | bytes 786440 | tf_op jit(solution)/shard_map/ppermute | solution.py:16
  182.7 9.7 %collective-permute-start.5 = (bf16[128,4,256]{2,0,1:T(8,128)(2,1)S(1)}, bf16[128,4,256]{2,0,1:T(8,128)(2,1)S(1)}, u32[]{:S(2)}, u32[]{:S(2)}) collective-permute-start(bf16[128,4,256]{2,0,1:T(8,128)(2,1)S(1)} %collective-permute-done.4), channel_id=1, source_target_pairs={{0,1},{1,2},{2,3},{3,4},{4,5},{5,6},{6,7},{7,8},{8,9},{9,10},{10,1... | collective-permute-start | bytes 786440 | tf_op jit(solution)/shard_map/ppermute | solution.py:16
  192.4 9.7 %collective-permute-start.6 = (bf16[128,4,256]{2,0,1:T(8,128)(2,1)S(1)}, bf16[128,4,256]{2,0,1:T(8,128)(2,1)S(1)}, u32[]{:S(2)}, u32[]{:S(2)}) collective-permute-start(bf16[128,4,256]{2,0,1:T(8,128)(2,1)S(1)} %collective-permute-done.5), channel_id=1, source_target_pairs={{0,1},{1,2},{2,3},{3,4},{4,5},{5,6},{6,7},{7,8},{8,9},{9,10},{10,1... | collective-permute-start | bytes 786440 | tf_op jit(solution)/shard_map/ppermute | solution.py:16
  202.2 9.8 %collective-permute-start.7 = (bf16[128,4,256]{2,0,1:T(8,128)(2,1)S(1)}, bf16[128,4,256]{2,0,1:T(8,128)(2,1)S(1)}, u32[]{:S(2)}, u32[]{:S(2)}) collective-permute-start(bf16[128,4,256]{2,0,1:T(8,128)(2,1)S(1)} %collective-permute-done.6), channel_id=1, source_target_pairs={{0,1},{1,2},{2,3},{3,4},{4,5},{5,6},{6,7},{7,8},{8,9},{9,10},{10,1... | collective-permute-start | bytes 786440 | tf_op jit(solution)/shard_map/ppermute | solution.py:16
  221.3 2.4 copy-start.1
  225.1 1.3 copy-start.2
  233.5 2.4 copy-start.1
  237.2 1.3 copy-start.2
  245.7 2.4 copy-start.1
  249.4 1.3 copy-start.2
  257.8 2.4 copy-start.1
  261.6 1.3 copy-start.2
  270.0 2.4 copy-start.1
  273.8 1.3 copy-start.2
  282.2 2.4 copy-start.1
  285.9 1.3 copy-start.2
  294.4 2.4 copy-start.1
  298.1 1.3 copy-start.2
  306.5 2.4 copy-start.1
  310.3 1.3 copy-start.2
  332.6 1.8 copy-start.3
  335.3 1.3 copy-start.4
  347.4 1.8 copy-start.3
  350.1 1.3 copy-start.4
  362.2 1.8 copy-start.3
  365.0 1.3 copy-start.4
  377.0 1.8 copy-start.3
  379.8 1.3 copy-start.4
  391.8 1.8 copy-start.3
  394.6 1.3 copy-start.4
  406.6 1.8 copy-start.3
  409.4 1.3 copy-start.4
  421.4 1.8 copy-start.3
  424.1 1.3 copy-start.4
  436.2 1.8 copy-start.3
  438.9 1.3 copy-start.4
  450.7 28.3 %collective-permute-start.8 = (f32[128,4,256]{0,2,1:T(8,128)S(1)}, f32[128,4,256]{0,2,1:T(8,128)S(1)}, u32[]{:S(2)}, u32[]{:S(2)}) collective-permute-start(f32[128,4,256]{0,2,1:T(8,128)S(1)} %slice_bitcast_fusion.9), channel_id=1, source_target_pairs={{1,0},{2,1},{3,2},{4,3},{5,4},{6,5},{7,6},{8,7},{9,8},{10,9},{11,1... | collective-permute-start | bytes 1572872 | tf_op jit(solution)/shard_map/ppermute | solution.py:16
  480.1 12.6 %collective-permute-start.9 = (f32[128,4,256]{0,2,1:T(8,128)S(1)}, f32[128,4,256]{0,2,1:T(8,128)S(1)}, u32[]{:S(2)}, u32[]{:S(2)}) collective-permute-start(f32[128,4,256]{0,2,1:T(8,128)S(1)} %bitcast_add_fusion.9), channel_id=1, source_target_pairs={{1,0},{2,1},{3,2},{4,3},{5,4},{6,5},{7,6},{8,7},{9,8},{10,9},{11,1... | collective-permute-start | bytes 1572872 | tf_op jit(solution)/shard_map/ppermute | solution.py:16
  493.9 12.6 %collective-permute-start.10 = (f32[128,4,256]{0,2,1:T(8,128)S(1)}, f32[128,4,256]{0,2,1:T(8,128)S(1)}, u32[]{:S(2)}, u32[]{:S(2)}) collective-permute-start(f32[128,4,256]{0,2,1:T(8,128)S(1)} %bitcast_add_fusion.8), channel_id=1, source_target_pairs={{1,0},{2,1},{3,2},{4,3},{5,4},{6,5},{7,6},{8,7},{9,8},{10,9},{11,1... | collective-permute-start | bytes 1572872 | tf_op jit(solution)/shard_map/ppermute | solution.py:16
  507.6 12.6 %collective-permute-start.11 = (f32[128,4,256]{0,2,1:T(8,128)S(1)}, f32[128,4,256]{0,2,1:T(8,128)S(1)}, u32[]{:S(2)}, u32[]{:S(2)}) collective-permute-start(f32[128,4,256]{0,2,1:T(8,128)S(1)} %bitcast_add_fusion.7), channel_id=1, source_target_pairs={{1,0},{2,1},{3,2},{4,3},{5,4},{6,5},{7,6},{8,7},{9,8},{10,9},{11,1... | collective-permute-start | bytes 1572872 | tf_op jit(solution)/shard_map/ppermute | solution.py:16
  521.3 12.6 %collective-permute-start.12 = (f32[128,4,256]{0,2,1:T(8,128)S(1)}, f32[128,4,256]{0,2,1:T(8,128)S(1)}, u32[]{:S(2)}, u32[]{:S(2)}) collective-permute-start(f32[128,4,256]{0,2,1:T(8,128)S(1)} %bitcast_add_fusion.6), channel_id=1, source_target_pairs={{1,0},{2,1},{3,2},{4,3},{5,4},{6,5},{7,6},{8,7},{9,8},{10,9},{11,1... | collective-permute-start | bytes 1572872 | tf_op jit(solution)/shard_map/ppermute | solution.py:16
  535.0 12.6 %collective-permute-start.13 = (f32[128,4,256]{0,2,1:T(8,128)S(1)}, f32[128,4,256]{0,2,1:T(8,128)S(1)}, u32[]{:S(2)}, u32[]{:S(2)}) collective-permute-start(f32[128,4,256]{0,2,1:T(8,128)S(1)} %bitcast_add_fusion.5), channel_id=1, source_target_pairs={{1,0},{2,1},{3,2},{4,3},{5,4},{6,5},{7,6},{8,7},{9,8},{10,9},{11,1... | collective-permute-start | bytes 1572872 | tf_op jit(solution)/shard_map/ppermute | solution.py:16
  548.8 19.0 %copy-start.5 = (f32[128,4,8,128]{3,0,2,1:T(8,128)S(1)}, f32[128,4,8,128]{3,0,2,1:T(8,128)}, u32[]{:S(2)}) copy-start(f32[128,4,8,128]{3,0,2,1:T(8,128)} %get-tuple-element.726) | copy-start | bytes 6291460
  548.8 12.7 %collective-permute-start.14 = (f32[128,4,256]{0,2,1:T(8,128)S(1)}, f32[128,4,256]{0,2,1:T(8,128)S(1)}, u32[]{:S(2)}, u32[]{:S(2)}) collective-permute-start(f32[128,4,256]{0,2,1:T(8,128)S(1)} %bitcast_add_fusion.4), channel_id=1, source_target_pairs={{1,0},{2,1},{3,2},{4,3},{5,4},{6,5},{7,6},{8,7},{9,8},{10,9},{11,1... | collective-permute-start | bytes 1572872 | tf_op jit(solution)/shard_map/ppermute | solution.py:16
  563.5 12.9 %collective-permute-start.15 = (f32[128,4,256]{0,2,1:T(8,128)}, f32[128,4,256]{0,2,1:T(8,128)}, u32[]{:S(2)}, u32[]{:S(2)}) collective-permute-start(f32[128,4,256]{0,2,1:T(8,128)} %bitcast_add_fusion.3), channel_id=1, source_target_pairs={{1,0},{2,1},{3,2},{4,3},{5,4},{6,5},{7,6},{8,7},{9,8},{10,9},{11,1... | collective-permute-start | bytes 1572872 | tf_op jit(solution)/shard_map/ppermute | solution.py:16
Sparse Core Ops, SparseCore 0:
  11.7 120.0 all-gather.1
where the time goes:
time: 595 us; the launch traced here: 592 us
  waiting for transfers between devices  235 us (39%)
  local copies, waits for them, and re-layouts  95.1 us (16%)
  other arithmetic  75.2 us (13%)
  starting transfers between devices  62.9 us (11%)
  matrix products  60.4 us (10%)
  loops' own time  48.7 us (8%)
  between operations  14.3 us (2%)
    all_gather x1, waiting for transfers between devices, shards(): lax.all_gather(key_value_weight, ('dp', 'ctx'), axis=0, tiled=True)  124 us
    ppermute x16, waiting for transfers between devices, from_behind(): lax.ppermute(value, axis, [(source, source + steps) for source in range(f...  111 us
    ppermute x16, starting transfers between devices, from_behind(): lax.ppermute(value, axis, [(source, source + steps) for source in range(f...  62.9 us
    cond x72, local copies, waits for them, and re-layouts  24.9 us
    another operation x1, loops' own time, attend(): lax.scan(backward_step, jnp.zeros(query_tile_block.shape, jnp.float32), (...  23.8 us
    another operation x1, loops' own time, attend(): state, unused = lax.scan(forward_step, state, (key_blocks, key_starts))  23.1 us
    dot_general x16, matrix products, scores(): jnp.einsum('qhgd,khd->hgqk', query_tile_block, block_slice[..., :width],...  19.2 us
    dynamic_update_slice x9, local copies, waits for them, and re-layouts, attend(): lax.scan(backward_step, jnp.zeros(query_tile_block.shape, jnp.float32), (...  17 us
  transfers between devices with their start and end apart: 17, of which 15 were waited for; matrix products, arithmetic and copies ran while one was open for 3% of the time, Pallas kernels for 0%

commit v1 on v0

--- a/solution.py
+++ b/solution.py
@@ -142,7 +142,12 @@
     half_length = columns_all // 2
     projected_input = jnp.dot(
         inputs,
-        lax.all_gather(key_value_weight, ("dp", "ctx"), axis=0, tiled=True),
+        jnp.concatenate(
+            lax.all_to_all(
+                jnp.stack([key_value_weight] * lax.axis_size(("dp", "ctx"))), ("dp", "ctx"), 0, 0
+            ),
+            axis=0,
+        ),
         preferred_element_type=jnp.float32,
     )
     projected_input = projected_input.astype(jnp.bfloat16)

time: 595 us -> 642 us (1.079)
  blocking collectives: 0 us -> 202 us
  waiting for transfers between devices: 235 us -> 110 us
  matrix products: 60.4 us -> 46.2 us
  local copies, waits for them, and re-layouts: 95.1 us -> 86.3 us
  other arithmetic: 75.2 us -> 66.6 us
    all_to_all x0 -> x1, blocking collectives: none -> 202 us  [shards(): lax.all_to_all(jnp.stack([key_value_weight] * lax.axis_size(('dp', 'ctx')...]
    all_gather x1, waiting for transfers between devices: 124 us -> 0.02 us  [shards(): lax.all_gather(key_value_weight, ('dp', 'ctx'), axis=0, tiled=True)]
    dot_general x16, matrix products: 19.2 us -> 8.17 us  [scores(): jnp.einsum('qhgd,khd->hgqk', query_tile_block, block_slice[..., :width],...]
    dynamic_update_slice x9, local copies, waits for them, and re-layouts: 17 us -> 7.67 us  [attend(): lax.scan(backward_step, jnp.zeros(query_tile_block.shape, jnp.float32), (...]
    unnamed x25 -> x29, local copies, waits for them, and re-layouts: 13.2 us -> 12.7 us
  transfers between devices with their start and end apart: 17 -> 17, of which waited for: 15 -> 14; matrix products, arithmetic and copies ran while one was open for 3% -> 26% of each run, Pallas kernels for 0% -> 0%
where the time goes in v1:
time: 642 us; the launch traced here: 639 us
  blocking collectives  202 us (31%)
  waiting for transfers between devices  110 us (17%)
  local copies, waits for them, and re-layouts  86.3 us (13%)
  other arithmetic  66.6 us (10%)
  starting transfers between devices  64.8 us (10%)
  loops' own time  48.2 us (8%)
  matrix products  46.2 us (7%)
  between operations  14.4 us (2%)
    all_to_all x1, blocking collectives, shards(): lax.all_to_all(jnp.stack([key_value_weight] * lax.axis_size(('dp', 'ctx')...  202 us
    ppermute x16, waiting for transfers between devices, from_behind(): lax.ppermute(value, axis, [(source, source + steps) for source in range(f...  110 us
    ppermute x16, starting transfers between devices, from_behind(): lax.ppermute(value, axis, [(source, source + steps) for source in range(f...  64.7 us
    cond x72, local copies, waits for them, and re-layouts  25.6 us
    another operation x1, loops' own time, attend(): state, unused = lax.scan(forward_step, state, (key_blocks, key_starts))  23.3 us
    another operation x1, loops' own time, attend(): lax.scan(backward_step, jnp.zeros(query_tile_block.shape, jnp.float32), (...  23.1 us
    squeeze x16, local copies, waits for them, and re-layouts, attend(): state, unused = lax.scan(forward_step, state, (key_blocks, key_starts))  16.7 us
    reduce_sum x36, other arithmetic, document_of(): return jnp.sum((positions[..., None] >= ends).astype(jnp.int32), axis=-1)  13.8 us
  transfers between devices with their start and end apart: 17, of which 14 were waited for; matrix products, arithmetic and copies ran while one was open for 26% of the time, Pallas kernels for 0%

profile of v1, /device:TPU:57, one launch (start us, length us, event | category | flops | bytes accessed | tf_op | source)
XLA Modules:
  0.0 638.5 jit_solution(15688969623759315300)
XLA Ops:
  7.2 1.9 stack.22
  9.1 201.6 %all_to_all.5 = bf16[256,16,1024]{2,1,0:T(8,128)(2,1)S(1)} all-to-all(bf16[256,16,1024]{2,1,0:T(8,128)(2,1)S(1)} %stack.22), channel_id=1, replica_groups=mesh['dp'=8,'ctx'=32] {'dp','ctx'}, dimensions={0} | all-to-all | bytes 16777216 | tf_op jit(solution)/shard_map/all_to_all | solution.py:146
  212.2 4.0 collective-permute-start
  216.2 3.3 collective-permute-done
  219.5 6.5 %collective-permute-start.1 = (bf16[128,4,256]{2,0,1:T(8,128)(2,1)S(1)}, bf16[128,4,256]{2,0,1:T(8,128)(2,1)S(1)}, u32[]{:S(2)}, u32[]{:S(2)}) collective-permute-start(bf16[128,4,256]{2,0,1:T(8,128)(2,1)S(1)} %collective-permute-done), channel_id=1, source_target_pairs={{0,1},{1,2},{2,3},{3,4},{4,5},{5,6},{6,7},{7,8},{8,9},{9,10},{10,1... | collective-permute-start | bytes 786440 | tf_op jit(solution)/shard_map/ppermute | solution.py:16
  226.0 3.3 collective-permute-done.1
  229.3 6.5 %collective-permute-start.2 = (bf16[128,4,256]{2,0,1:T(8,128)(2,1)S(1)}, bf16[128,4,256]{2,0,1:T(8,128)(2,1)}, u32[]{:S(2)}, u32[]{:S(2)}) collective-permute-start(bf16[128,4,256]{2,0,1:T(8,128)(2,1)S(1)} %collective-permute-done.1), channel_id=1, source_target_pairs={{0,1},{1,2},{2,3},{3,4},{4,5},{5,6},{6,7},{7,8},{8,9},{9,10},{10,1... | collective-permute-start | bytes 786440 | tf_op jit(solution)/shard_map/ppermute | solution.py:16
  235.8 3.3 collective-permute-done.2
  239.1 6.6 %collective-permute-start.3 = (bf16[128,4,256]{2,0,1:T(8,128)(2,1)}, bf16[128,4,256]{2,0,1:T(8,128)(2,1)}, u32[]{:S(2)}, u32[]{:S(2)}) collective-permute-start(bf16[128,4,256]{2,0,1:T(8,128)(2,1)} %collective-permute-done.2), channel_id=1, source_target_pairs={{0,1},{1,2},{2,3},{3,4},{4,5},{5,6},{6,7},{7,8},{8,9},{9,10},{10,1... | collective-permute-start | bytes 786440 | tf_op jit(solution)/shard_map/ppermute | solution.py:16
  247.4 1.6 copy.51
  249.7 6.2 collective-permute-start.4
  256.7 1.7 bitcast_dynamic-update-slice_fusion.7
  259.6 6.4 collective-permute-start.5
  266.0 1.7 bitcast_dynamic-update-slice_fusion.6
  267.6 1.7 bitcast_dynamic-update-slice_fusion.5
  269.3 6.4 %collective-permute-start.6 = (bf16[128,4,256]{2,0,1:T(8,128)(2,1)S(1)}, bf16[128,4,256]{2,0,1:T(8,128)(2,1)S(1)}, u32[]{:S(2)}, u32[]{:S(2)}) collective-permute-start(bf16[128,4,256]{2,0,1:T(8,128)(2,1)S(1)} %collective-permute-done.5), channel_id=1, source_target_pairs={{0,1},{1,2},{2,3},{3,4},{4,5},{5,6},{6,7},{7,8},{8,9},{9,10},{10,1... | collective-permute-start | bytes 786440 | tf_op jit(solution)/shard_map/ppermute | solution.py:16
  275.7 1.7 bitcast_dynamic-update-slice_fusion.4
  279.0 6.5 %collective-permute-start.7 = (bf16[128,4,256]{2,0,1:T(8,128)(2,1)S(1)}, bf16[128,4,256]{2,0,1:T(8,128)(2,1)S(1)}, u32[]{:S(2)}, u32[]{:S(2)}) collective-permute-start(bf16[128,4,256]{2,0,1:T(8,128)(2,1)S(1)} %collective-permute-done.6), channel_id=1, source_target_pairs={{0,1},{1,2},{2,3},{3,4},{4,5},{5,6},{6,7},{7,8},{8,9},{9,10},{10,1... | collective-permute-start | bytes 786440 | tf_op jit(solution)/shard_map/ppermute | solution.py:16
  287.0 2.3 collective-permute-done.7
  290.0 1.5 broadcast.103.clone
  291.6 88.1 %while.39 = (s32[]{:T(128)}, f32[4,8,128]{2,1,0:T(8,128)S(1)}, f32[4,8,128]{2,1,0:T(8,128)S(1)}, f32[128,4,8,128]{3,0,2,1:T(8,128)}, s32[9]{0:T(128)S(1)}, /*ind...) while((s32[]{:T(128)}, f32[4,8,128]{2,1,0:T(8,128)S(1)}, ...), condition=%wide.region_10.11_spmd.clone, body=%wide.region_3.10_spmd.clone.sunk | while | flops 275341920 | bytes 29466568 | solution.py:87
  296.1 5.9 conditional.6
  299.3 1.4 bitcast_add_fusion
  306.5 5.9 conditional.6
  309.7 1.4 bitcast_add_fusion
  316.9 5.9 conditional.6
  320.1 1.4 bitcast_add_fusion
  327.4 6.0 conditional.6
  337.9 5.9 conditional.6
  341.1 1.4 bitcast_add_fusion
  348.4 5.9 conditional.6
  351.5 1.4 bitcast_add_fusion
  358.8 5.9 conditional.6
  362.0 1.4 bitcast_add_fusion
  369.2 5.9 conditional.6
  379.7 2.9 copy.49
  382.6 3.1 multiply_reduce_fusion
  385.7 1.5 broadcast.103
  387.2 111.6 %while.40 = (s32[]{:T(128)}, f32[128,4,8,128]{3,0,2,1:T(8,128)}, f32[9,128,4,256]{1,3,2,0:T(8,128)}, s32[9]{0:T(128)S(1)}, s32[]{:T(128)}, /*index=5*/s32[32]{0:...) while((s32[]{:T(128)}, f32[128,4,8,128]{3,0,2,1:T(8,128)}, ...), condition=%wide.region_17.18_spmd.clone, body=%wide.region_12.17_spmd.clone.sunk | while | flops 675558016 | bytes 38248888 | solution.py:131
  391.7 7.9 %conditional.7 = (f32[128,4,8,128]{3,0,2,1:T(8,128)}, f32[1,128,4,256]{1,3,2,0:T(8,128)S(1)}) conditional(s32[]{:T(128)} %convert_element_type.146, f32[128,4,8,128]{3,0,2,1:T(8,128)} %get-tuple-element.1136, (s32[128]{0:T(128)S(1)}, s32[128,32]{1,0:T(8,128)S(1)}, s32[]{:T(128)}, s32[1,128]{1,0:T(1,128)S(1)}, s32[]{:T(128)}, ...), branch_computations={%region_14.14_spmd, %region_15.16_spmd} | conditional | flops 675549568 | bytes 37180764 | solution.py:129
  405.0 7.9 %conditional.7 = (f32[128,4,8,128]{3,0,2,1:T(8,128)}, f32[1,128,4,256]{1,3,2,0:T(8,128)S(1)}) conditional(s32[]{:T(128)} %convert_element_type.146, f32[128,4,8,128]{3,0,2,1:T(8,128)} %get-tuple-element.1136, (s32[128]{0:T(128)S(1)}, s32[128,32]{1,0:T(8,128)S(1)}, s32[]{:T(128)}, s32[1,128]{1,0:T(1,128)S(1)}, s32[]{:T(128)}, ...), branch_computations={%region_14.14_spmd, %region_15.16_spmd} | conditional | flops 675549568 | bytes 37180764 | solution.py:129
  418.4 7.9 %conditional.7 = (f32[128,4,8,128]{3,0,2,1:T(8,128)}, f32[1,128,4,256]{1,3,2,0:T(8,128)S(1)}) conditional(s32[]{:T(128)} %convert_element_type.146, f32[128,4,8,128]{3,0,2,1:T(8,128)} %get-tuple-element.1136, (s32[128]{0:T(128)S(1)}, s32[128,32]{1,0:T(8,128)S(1)}, s32[]{:T(128)}, s32[1,128]{1,0:T(1,128)S(1)}, s32[]{:T(128)}, ...), branch_computations={%region_14.14_spmd, %region_15.16_spmd} | conditional | flops 675549568 | bytes 37180764 | solution.py:129
  431.6 7.9 %conditional.7 = (f32[128,4,8,128]{3,0,2,1:T(8,128)}, f32[1,128,4,256]{1,3,2,0:T(8,128)S(1)}) conditional(s32[]{:T(128)} %convert_element_type.146, f32[128,4,8,128]{3,0,2,1:T(8,128)} %get-tuple-element.1136, (s32[128]{0:T(128)S(1)}, s32[128,32]{1,0:T(8,128)S(1)}, s32[]{:T(128)}, s32[1,128]{1,0:T(1,128)S(1)}, s32[]{:T(128)}, ...), branch_computations={%region_14.14_spmd, %region_15.16_spmd} | conditional | flops 675549568 | bytes 37180764 | solution.py:129
  444.9 7.9 %conditional.7 = (f32[128,4,8,128]{3,0,2,1:T(8,128)}, f32[1,128,4,256]{1,3,2,0:T(8,128)S(1)}) conditional(s32[]{:T(128)} %convert_element_type.146, f32[128,4,8,128]{3,0,2,1:T(8,128)} %get-tuple-element.1136, (s32[128]{0:T(128)S(1)}, s32[128,32]{1,0:T(8,128)S(1)}, s32[]{:T(128)}, s32[1,128]{1,0:T(1,128)S(1)}, s32[]{:T(128)}, ...), branch_computations={%region_14.14_spmd, %region_15.16_spmd} | conditional | flops 675549568 | bytes 37180764 | solution.py:129
  458.2 7.9 %conditional.7 = (f32[128,4,8,128]{3,0,2,1:T(8,128)}, f32[1,128,4,256]{1,3,2,0:T(8,128)S(1)}) conditional(s32[]{:T(128)} %convert_element_type.146, f32[128,4,8,128]{3,0,2,1:T(8,128)} %get-tuple-element.1136, (s32[128]{0:T(128)S(1)}, s32[128,32]{1,0:T(8,128)S(1)}, s32[]{:T(128)}, s32[1,128]{1,0:T(1,128)S(1)}, s32[]{:T(128)}, ...), branch_computations={%region_14.14_spmd, %region_15.16_spmd} | conditional | flops 675549568 | bytes 37180764 | solution.py:129
  471.4 7.9 %conditional.7 = (f32[128,4,8,128]{3,0,2,1:T(8,128)}, f32[1,128,4,256]{1,3,2,0:T(8,128)S(1)}) conditional(s32[]{:T(128)} %convert_element_type.146, f32[128,4,8,128]{3,0,2,1:T(8,128)} %get-tuple-element.1136, (s32[128]{0:T(128)S(1)}, s32[128,32]{1,0:T(8,128)S(1)}, s32[]{:T(128)}, s32[1,128]{1,0:T(1,128)S(1)}, s32[]{:T(128)}, ...), branch_computations={%region_14.14_spmd, %region_15.16_spmd} | conditional | flops 675549568 | bytes 37180764 | solution.py:129
  484.7 7.9 %conditional.7 = (f32[128,4,8,128]{3,0,2,1:T(8,128)}, f32[1,128,4,256]{1,3,2,0:T(8,128)S(1)}) conditional(s32[]{:T(128)} %convert_element_type.146, f32[128,4,8,128]{3,0,2,1:T(8,128)} %get-tuple-element.1136, (s32[128]{0:T(128)S(1)}, s32[128,32]{1,0:T(8,128)S(1)}, s32[]{:T(128)}, s32[1,128]{1,0:T(1,128)S(1)}, s32[]{:T(128)}, ...), branch_computations={%region_14.14_spmd, %region_15.16_spmd} | conditional | flops 675549568 | bytes 37180764 | solution.py:129
  499.9 2.1 collective-permute-start.8
  502.0 25.0 %collective-permute-done.8 = f32[128,4,256]{0,2,1:T(8,128)S(1)} collective-permute-done((f32[128,4,256]{0,2,1:T(8,128)S(1)}, f32[128,4,256]{0,2,1:T(8,128)S(1)}, u32[]{:S(2)}, u32[]{:S(2)}) %collective-permute-start.8) | collective-permute-done | bytes 524320 | tf_op jit(solution)/shard_map/ppermute | solution.py:16
  528.1 1.9 collective-permute-start.9
  530.0 10.7 %collective-permute-done.9 = f32[128,4,256]{0,2,1:T(8,128)S(1)} collective-permute-done((f32[128,4,256]{0,2,1:T(8,128)S(1)}, f32[128,4,256]{0,2,1:T(8,128)S(1)}, u32[]{:S(2)}, u32[]{:S(2)}) %collective-permute-start.9) | collective-permute-done | bytes 524320 | tf_op jit(solution)/shard_map/ppermute | solution.py:16
  541.8 1.9 collective-permute-start.10
  543.7 10.7 %collective-permute-done.10 = f32[128,4,256]{0,2,1:T(8,128)S(1)} collective-permute-done((f32[128,4,256]{0,2,1:T(8,128)S(1)}, f32[128,4,256]{0,2,1:T(8,128)S(1)}, u32[]{:S(2)}, u32[]{:S(2)}) %collective-permute-start.10) | collective-permute-done | bytes 524320 | tf_op jit(solution)/shard_map/ppermute | solution.py:16
  555.5 1.9 collective-permute-start.11
  557.4 10.7 %collective-permute-done.11 = f32[128,4,256]{0,2,1:T(8,128)S(1)} collective-permute-done((f32[128,4,256]{0,2,1:T(8,128)S(1)}, f32[128,4,256]{0,2,1:T(8,128)S(1)}, u32[]{:S(2)}, u32[]{:S(2)}) %collective-permute-start.11) | collective-permute-done | bytes 524320 | tf_op jit(solution)/shard_map/ppermute | solution.py:16
  569.2 2.1 collective-permute-start.12
  571.3 10.7 %collective-permute-done.12 = f32[128,4,256]{0,2,1:T(8,128)S(1)} collective-permute-done((f32[128,4,256]{0,2,1:T(8,128)S(1)}, f32[128,4,256]{0,2,1:T(8,128)S(1)}, u32[]{:S(2)}, u32[]{:S(2)}) %collective-permute-start.12) | collective-permute-done | bytes 524320 | tf_op jit(solution)/shard_map/ppermute | solution.py:16
  583.1 1.9 collective-permute-start.13
  585.0 10.7 %collective-permute-done.13 = f32[128,4,256]{0,2,1:T(8,128)S(1)} collective-permute-done((f32[128,4,256]{0,2,1:T(8,128)S(1)}, f32[128,4,256]{0,2,1:T(8,128)S(1)}, u32[]{:S(2)}, u32[]{:S(2)}) %collective-permute-start.13) | collective-permute-done | bytes 524320 | tf_op jit(solution)/shard_map/ppermute | solution.py:16
  596.8 1.9 collective-permute-start.14
  598.8 10.7 %collective-permute-done.14 = f32[128,4,256]{0,2,1:T(8,128)S(1)} collective-permute-done((f32[128,4,256]{0,2,1:T(8,128)S(1)}, f32[128,4,256]{0,2,1:T(8,128)S(1)}, u32[]{:S(2)}, u32[]{:S(2)}) %collective-permute-start.14) | collective-permute-done | bytes 524320 | tf_op jit(solution)/shard_map/ppermute | solution.py:16
  610.6 1.9 collective-permute-start.15
  616.1 7.1 %collective-permute-done.15 = f32[128,4,256]{0,2,1:T(8,128)S(1)} collective-permute-done((f32[128,4,256]{0,2,1:T(8,128)S(1)}, f32[128,4,256]{0,2,1:T(8,128)S(1)}, u32[]{:S(2)}, u32[]{:S(2)}) %collective-permute-start.15) | collective-permute-done | bytes 524320 | tf_op jit(solution)/shard_map/ppermute | solution.py:16
  624.3 7.3 %fusion.27 = bf16[1,128,4096]{2,1,0:T(8,128)(2,1)} fusion(bf16[4096,1024]{1,0:T(8,128)(2,1)} %all-gather.2.cloned.1.call-done, bf16[128,512]{0,1:T(8,128)(2,1)S(1)} %bitcast.169, bf16[128,512]{0,1:T(8,128)(2,1)S(1)} %bitcast.168), kind=kOutput, calls=%fused_computation.57 | convolution fusion | flops 1074790400 | bytes 9699328 | tf_op jit(solution)/shard_map/dot_general | solution.py:184
  (429 shorter events, 166.6 us)
Async XLA Ops:
  7.2 203.6 %copy-start = (bf16[1,128,4096]{2,1,0:T(8,128)(2,1)S(1)}, bf16[1,128,4096]{2,1,0:T(8,128)(2,1)}, u32[]{:S(2)}) copy-start(bf16[1,128,4096]{2,1,0:T(8,128)(2,1)} %param.14) | copy-start | bytes 3145732
  7.2 617.1 %all-gather.2.cloned.1.call-start = ((), (), s32[]{:S(2)}) async-start(), calls=%async_computation.1 | async-start | bytes 8421376 | tf_op jit(solution)/shard_map/all_gather | solution.py:186
  210.7 35.0 %copy-start.11 = (s32[1,32]{1,0:T(1,128)S(1)}, s32[1,32]{1,0:T(1,128)}, u32[]{:S(2)}) copy-start(s32[1,32]{1,0:T(1,128)} %param.17) | copy-start | bytes 388
  210.7 35.3 %copy-start.8 = (bf16[1,128,4096]{2,1,0:T(8,128)(2,1)S(1)}, bf16[1,128,4096]{2,1,0:T(8,128)(2,1)}, u32[]{:S(2)}) copy-start(bf16[1,128,4096]{2,1,0:T(8,128)(2,1)} %param.13) | copy-start | bytes 3145732
  212.2 7.3 %collective-permute-start = (bf16[128,4,256]{2,0,1:T(8,128)(2,1)S(1)}, bf16[128,4,256]{2,0,1:T(8,128)(2,1)S(1)}, u32[]{:S(2)}, u32[]{:S(2)}) collective-permute-start(bf16[128,4,256]{2,0,1:T(8,128)(2,1)S(1)} %bitcast_dynamic-update-slice_fusion.9), channel_id=1, source_target_pairs={{0,1},{1,2},{2,3},{3,4},{4,5},{5,6},{6,7},{7,8},{8,9},{9,10},{10,1... | collective-permute-start | bytes 786440 | tf_op jit(solution)/shard_map/ppermute | solution.py:16
  219.5 26.5 %copy-start.10 = (bf16[128,4,256]{2,0,1:T(8,128)(2,1)}, bf16[128,4,256]{2,0,1:T(8,128)(2,1)S(1)}, u32[]{:S(2)}) copy-start(bf16[128,4,256]{2,0,1:T(8,128)(2,1)S(1)} %collective-permute-done) | copy-start | bytes 786436
  219.5 9.8 %collective-permute-start.1 = (bf16[128,4,256]{2,0,1:T(8,128)(2,1)S(1)}, bf16[128,4,256]{2,0,1:T(8,128)(2,1)S(1)}, u32[]{:S(2)}, u32[]{:S(2)}) collective-permute-start(bf16[128,4,256]{2,0,1:T(8,128)(2,1)S(1)} %collective-permute-done), channel_id=1, source_target_pairs={{0,1},{1,2},{2,3},{3,4},{4,5},{5,6},{6,7},{7,8},{8,9},{9,10},{10,1... | collective-permute-start | bytes 786440 | tf_op jit(solution)/shard_map/ppermute | solution.py:16
  229.3 16.7 %copy-start.9 = (bf16[128,4,256]{2,0,1:T(8,128)(2,1)}, bf16[128,4,256]{2,0,1:T(8,128)(2,1)S(1)}, u32[]{:S(2)}) copy-start(bf16[128,4,256]{2,0,1:T(8,128)(2,1)S(1)} %collective-permute-done.1) | copy-start | bytes 786436
  229.3 9.8 %collective-permute-start.2 = (bf16[128,4,256]{2,0,1:T(8,128)(2,1)S(1)}, bf16[128,4,256]{2,0,1:T(8,128)(2,1)}, u32[]{:S(2)}, u32[]{:S(2)}) collective-permute-start(bf16[128,4,256]{2,0,1:T(8,128)(2,1)S(1)} %collective-permute-done.1), channel_id=1, source_target_pairs={{0,1},{1,2},{2,3},{3,4},{4,5},{5,6},{6,7},{7,8},{8,9},{9,10},{10,1... | collective-permute-start | bytes 786440 | tf_op jit(solution)/shard_map/ppermute | solution.py:16
  239.1 10.6 %collective-permute-start.3 = (bf16[128,4,256]{2,0,1:T(8,128)(2,1)}, bf16[128,4,256]{2,0,1:T(8,128)(2,1)}, u32[]{:S(2)}, u32[]{:S(2)}) collective-permute-start(bf16[128,4,256]{2,0,1:T(8,128)(2,1)} %collective-permute-done.2), channel_id=1, source_target_pairs={{0,1},{1,2},{2,3},{3,4},{4,5},{5,6},{6,7},{7,8},{8,9},{9,10},{10,1... | collective-permute-start | bytes 786440 | tf_op jit(solution)/shard_map/ppermute | solution.py:16
  249.7 9.9 %collective-permute-start.4 = (bf16[128,4,256]{2,0,1:T(8,128)(2,1)}, bf16[128,4,256]{2,0,1:T(8,128)(2,1)S(1)}, u32[]{:S(2)}, u32[]{:S(2)}) collective-permute-start(bf16[128,4,256]{2,0,1:T(8,128)(2,1)} %collective-permute-done.3), channel_id=1, source_target_pairs={{0,1},{1,2},{2,3},{3,4},{4,5},{5,6},{6,7},{7,8},{8,9},{9,10},{10,1... | collective-permute-start | bytes 786440 | tf_op jit(solution)/shard_map/ppermute | solution.py:16
  259.6 9.8 %collective-permute-start.5 = (bf16[128,4,256]{2,0,1:T(8,128)(2,1)S(1)}, bf16[128,4,256]{2,0,1:T(8,128)(2,1)S(1)}, u32[]{:S(2)}, u32[]{:S(2)}) collective-permute-start(bf16[128,4,256]{2,0,1:T(8,128)(2,1)S(1)} %collective-permute-done.4), channel_id=1, source_target_pairs={{0,1},{1,2},{2,3},{3,4},{4,5},{5,6},{6,7},{7,8},{8,9},{9,10},{10,1... | collective-permute-start | bytes 786440 | tf_op jit(solution)/shard_map/ppermute | solution.py:16
  269.3 9.7 %collective-permute-start.6 = (bf16[128,4,256]{2,0,1:T(8,128)(2,1)S(1)}, bf16[128,4,256]{2,0,1:T(8,128)(2,1)S(1)}, u32[]{:S(2)}, u32[]{:S(2)}) collective-permute-start(bf16[128,4,256]{2,0,1:T(8,128)(2,1)S(1)} %collective-permute-done.5), channel_id=1, source_target_pairs={{0,1},{1,2},{2,3},{3,4},{4,5},{5,6},{6,7},{7,8},{8,9},{9,10},{10,1... | collective-permute-start | bytes 786440 | tf_op jit(solution)/shard_map/ppermute | solution.py:16
  279.0 10.2 %collective-permute-start.7 = (bf16[128,4,256]{2,0,1:T(8,128)(2,1)S(1)}, bf16[128,4,256]{2,0,1:T(8,128)(2,1)S(1)}, u32[]{:S(2)}, u32[]{:S(2)}) collective-permute-start(bf16[128,4,256]{2,0,1:T(8,128)(2,1)S(1)} %collective-permute-done.6), channel_id=1, source_target_pairs={{0,1},{1,2},{2,3},{3,4},{4,5},{5,6},{6,7},{7,8},{8,9},{9,10},{10,1... | collective-permute-start | bytes 786440 | tf_op jit(solution)/shard_map/ppermute | solution.py:16
  297.5 1.7 copy-start.2
  300.6 1.3 copy-start.3
  308.0 1.7 copy-start.2
  311.1 1.3 copy-start.3
  318.4 1.7 copy-start.2
  321.5 1.3 copy-start.3
  328.8 1.8 copy-start.2
  332.1 1.3 copy-start.3
  339.4 1.7 copy-start.2
  342.5 1.3 copy-start.3
  349.8 1.7 copy-start.2
  352.9 1.3 copy-start.3
  360.2 1.7 copy-start.2
  363.3 1.3 copy-start.3
  370.7 1.7 copy-start.2
  373.8 1.3 copy-start.3
  395.8 1.6 copy-start.4
  398.3 1.3 copy-start.5
  409.1 1.6 copy-start.4
  411.6 1.3 copy-start.5
  422.4 1.6 copy-start.4
  425.0 1.3 copy-start.5
  435.6 1.6 copy-start.4
  438.2 1.3 copy-start.5
  448.9 1.6 copy-start.4
  451.5 1.3 copy-start.5
  462.2 1.6 copy-start.4
  464.8 1.3 copy-start.5
  475.4 1.6 copy-start.4
  478.0 1.3 copy-start.5
  488.7 1.6 copy-start.4
  491.3 1.3 copy-start.5
  499.9 27.1 %collective-permute-start.8 = (f32[128,4,256]{0,2,1:T(8,128)S(1)}, f32[128,4,256]{0,2,1:T(8,128)S(1)}, u32[]{:S(2)}, u32[]{:S(2)}) collective-permute-start(f32[128,4,256]{0,2,1:T(8,128)S(1)} %slice_bitcast_fusion.9), channel_id=1, source_target_pairs={{1,0},{2,1},{3,2},{4,3},{5,4},{6,5},{7,6},{8,7},{9,8},{10,9},{11,1... | collective-permute-start | bytes 1572872 | tf_op jit(solution)/shard_map/ppermute | solution.py:16
  528.1 12.6 %collective-permute-start.9 = (f32[128,4,256]{0,2,1:T(8,128)S(1)}, f32[128,4,256]{0,2,1:T(8,128)S(1)}, u32[]{:S(2)}, u32[]{:S(2)}) collective-permute-start(f32[128,4,256]{0,2,1:T(8,128)S(1)} %bitcast_add_fusion.9), channel_id=1, source_target_pairs={{1,0},{2,1},{3,2},{4,3},{5,4},{6,5},{7,6},{8,7},{9,8},{10,9},{11,1... | collective-permute-start | bytes 1572872 | tf_op jit(solution)/shard_map/ppermute | solution.py:16
  541.8 12.6 %collective-permute-start.10 = (f32[128,4,256]{0,2,1:T(8,128)S(1)}, f32[128,4,256]{0,2,1:T(8,128)S(1)}, u32[]{:S(2)}, u32[]{:S(2)}) collective-permute-start(f32[128,4,256]{0,2,1:T(8,128)S(1)} %bitcast_add_fusion.8), channel_id=1, source_target_pairs={{1,0},{2,1},{3,2},{4,3},{5,4},{6,5},{7,6},{8,7},{9,8},{10,9},{11,1... | collective-permute-start | bytes 1572872 | tf_op jit(solution)/shard_map/ppermute | solution.py:16
  555.5 12.6 %collective-permute-start.11 = (f32[128,4,256]{0,2,1:T(8,128)S(1)}, f32[128,4,256]{0,2,1:T(8,128)S(1)}, u32[]{:S(2)}, u32[]{:S(2)}) collective-permute-start(f32[128,4,256]{0,2,1:T(8,128)S(1)} %bitcast_add_fusion.7), channel_id=1, source_target_pairs={{1,0},{2,1},{3,2},{4,3},{5,4},{6,5},{7,6},{8,7},{9,8},{10,9},{11,1... | collective-permute-start | bytes 1572872 | tf_op jit(solution)/shard_map/ppermute | solution.py:16
  569.2 43.3 %copy-start.6 = (f32[128,4,8,128]{3,0,2,1:T(8,128)S(1)}, f32[128,4,8,128]{3,0,2,1:T(8,128)}, u32[]{:S(2)}) copy-start(f32[128,4,8,128]{3,0,2,1:T(8,128)} %get-tuple-element.726) | copy-start | bytes 6291460
  569.2 12.7 %collective-permute-start.12 = (f32[128,4,256]{0,2,1:T(8,128)S(1)}, f32[128,4,256]{0,2,1:T(8,128)S(1)}, u32[]{:S(2)}, u32[]{:S(2)}) collective-permute-start(f32[128,4,256]{0,2,1:T(8,128)S(1)} %bitcast_add_fusion.6), channel_id=1, source_target_pairs={{1,0},{2,1},{3,2},{4,3},{5,4},{6,5},{7,6},{8,7},{9,8},{10,9},{11,1... | collective-permute-start | bytes 1572872 | tf_op jit(solution)/shard_map/ppermute | solution.py:16
  583.1 12.6 %collective-permute-start.13 = (f32[128,4,256]{0,2,1:T(8,128)S(1)}, f32[128,4,256]{0,2,1:T(8,128)S(1)}, u32[]{:S(2)}, u32[]{:S(2)}) collective-permute-start(f32[128,4,256]{0,2,1:T(8,128)S(1)} %bitcast_add_fusion.5), channel_id=1, source_target_pairs={{1,0},{2,1},{3,2},{4,3},{5,4},{6,5},{7,6},{8,7},{9,8},{10,9},{11,1... | collective-permute-start | bytes 1572872 | tf_op jit(solution)/shard_map/ppermute | solution.py:16
  596.8 12.6 %collective-permute-start.14 = (f32[128,4,256]{0,2,1:T(8,128)S(1)}, f32[128,4,256]{0,2,1:T(8,128)S(1)}, u32[]{:S(2)}, u32[]{:S(2)}) collective-permute-start(f32[128,4,256]{0,2,1:T(8,128)S(1)} %bitcast_add_fusion.4), channel_id=1, source_target_pairs={{1,0},{2,1},{3,2},{4,3},{5,4},{6,5},{7,6},{8,7},{9,8},{10,9},{11,1... | collective-permute-start | bytes 1572872 | tf_op jit(solution)/shard_map/ppermute | solution.py:16
  610.6 12.6 %collective-permute-start.15 = (f32[128,4,256]{0,2,1:T(8,128)S(1)}, f32[128,4,256]{0,2,1:T(8,128)S(1)}, u32[]{:S(2)}, u32[]{:S(2)}) collective-permute-start(f32[128,4,256]{0,2,1:T(8,128)S(1)} %bitcast_add_fusion.3), channel_id=1, source_target_pairs={{1,0},{2,1},{3,2},{4,3},{5,4},{6,5},{7,6},{8,7},{9,8},{10,9},{11,1... | collective-permute-start | bytes 1572872 | tf_op jit(solution)/shard_map/ppermute | solution.py:16
  612.8 2.0 copy-start.7
  624.3 7.4 %copy-start.1 = (bf16[1,128,4096]{2,1,0:T(8,128)(2,1)S(1)}, bf16[1,128,4096]{2,1,0:T(8,128)(2,1)}, u32[]{:S(2)}) copy-start(bf16[1,128,4096]{2,1,0:T(8,128)(2,1)} %param.14) | copy-start | bytes 3145732
Sparse Core Ops, SparseCore 0:
  235.9 112.7 all-gather.1
